TPU v7x, 128 devices: a whole 4x4x4 slice. The times are simulated.
128 devices in a mesh: dp: 32 (over x, y, core), tensor: 4 (over z).
Axes of the slice: x: 4, y: 4, z: 4, core: 2. Of those that a mesh axis runs over, the one named last changes fastest.
Arguments:
- activations: bfloat16 [65536, 8192], P('dp', 'tensor'), may hold values from -16 to 16
- whitening: bfloat16 [8192, 1024], P('tensor'), may hold values from -8 to 8
- factor: bfloat16 [1024, 1024], P(('dp', 'tensor')), may hold values from -2 to 2
Outputs:
- new_factor: float32 [1024, 1024], P(('dp', 'tensor'))
All inputs are finite; a program needn't handle non-finite values.
Results may differ from a plain program's by a relative error of at most 0.029.
Values may be sent and summed in bfloat16 or wider, within the bound.
A program may use at most 192 MiB of HBM per device.

v0:
```python
import jax
import jax.numpy as jnp
from jax import lax
from jax.sharding import PartitionSpec as P

ridge_shift = 0.1
epsilon = 1e-06


def solve_rows(moment_rows, hadamard):
    lower = jnp.linalg.cholesky(hadamard)
    first = jax.scipy.linalg.solve_triangular(lower, moment_rows.T, lower=True)
    second = jax.scipy.linalg.solve_triangular(lower, first, lower=True, trans=1)
    return second.T


def shards(activations, whitening, factor):
    summed = lax.psum_scatter(
        jnp.dot(activations, whitening, preferred_element_type=jnp.float32).astype(jnp.bfloat16),
        "tensor",
        scatter_dimension=0,
        tiled=True,
    )
    whole_factor = lax.all_gather(factor, ("dp", "tensor"), axis=0, tiled=True)
    projected = jnp.dot(summed, whole_factor, preferred_element_type=jnp.float32)
    squared = (projected * projected).astype(jnp.bfloat16)
    moment_rows = lax.psum_scatter(
        lax.dot_general(
            summed, squared, (((0,), (0,)), ((), ())), preferred_element_type=jnp.float32
        ),
        ("dp", "tensor"),
        scatter_dimension=0,
        tiled=True,
    )
    gram = jnp.dot(whole_factor.T, whole_factor, preferred_element_type=jnp.float32)
    hadamard = gram * gram + ridge_shift * jnp.eye(gram.shape[0], dtype=jnp.float32)
    updated = solve_rows(moment_rows, hadamard)
    column_total = lax.psum(jnp.sum(updated * updated, axis=0), ("dp", "tensor"))
    scale = jnp.sqrt(column_total / whole_factor.shape[0] + epsilon)
    return updated / scale[None, :]


def solution(mesh):
    placed = (P("dp", "tensor"), P("tensor", None), P(("dp", "tensor"), None))
    return jax.shard_map(
        shards, mesh=mesh, in_specs=placed, out_specs=P(("dp", "tensor"), None), check_vma=False
    )
```

profile of v0, /device:TPU:1, one launch (start us, length us, event | category | flops | bytes accessed | tf_op | source)
XLA Modules:
  0.0 901.7 jit_solution(2923321162316526728)
XLA Ops:
  8.1 13.8 %convolution_convert_fusion = bf16[2048,1024]{1,0:T(8,128)(2,1)} fusion(bf16[2048,2048]{1,0:T(8,128)(2,1)} %param.3, bf16[2048,1024]{1,0:T(8,128)(2,1)} %param.4), kind=kOutput, calls=%fused_computation.8 | convolution fusion | flops 8592031744 | bytes 16777216 | tf_op jit(solution)/shard_map/dot_general | solution.py:19
  22.0 77.6 %all-gather.2.cloned.1.call-done = bf16[1024,1024]{1,0:T(8,128)(2,1)} async-done(((bf16[8,1024]{1,0:T(8,128)(2,1)}), bf16[1024,1024]{1,0:T(8,128)(2,1)}) %all-gather.2.cloned.1.call-update) | async-done | bytes 2097168 | tf_op jit(solution)/shard_map/all_gather | solution.py:24
  108.6 5.8 copy.4
  120.9 11.7 %cholesky.222 = f32[128,128]{1,0:T(8,128)S(1)} custom-call(f32[128,128]{1,0:T(8,128)S(1)} %cholesky.577), custom_call_target="Cholesky" | custom-call | tf_op jit(solution)/shard_map/jit(cholesky)/cholesky | solution.py:11
  135.1 9.8 %custom-call.66 = f32[1,128,128]{1,2,0:T(8,128)S(1)} custom-call(f32[1,128,128]{2,1,0:T(8,128)S(1)} %get-tuple-element.44), custom_call_target="InvertDiagBlocksLowerTriangular" | custom-call | tf_op jit(solution)/shard_map/jit(cholesky)/cholesky | solution.py:11
  148.8 11.8 %cholesky.243 = f32[128,128]{1,0:T(8,128)S(1)} custom-call(f32[128,128]{1,0:T(8,128)S(1)} %cholesky.581), custom_call_target="Cholesky" | custom-call | tf_op jit(solution)/shard_map/jit(cholesky)/cholesky | solution.py:11
  160.7 5.9 fusion.1
  167.3 9.8 %custom-call.67 = f32[1,128,128]{1,2,0:T(8,128)S(1)} custom-call(f32[1,128,128]{2,1,0:T(8,128)S(1)} %get-tuple-element.41), custom_call_target="InvertDiagBlocksLowerTriangular" | custom-call | tf_op jit(solution)/shard_map/jit(cholesky)/cholesky | solution.py:11
  180.4 11.7 %cholesky.466 = f32[128,128]{1,0:T(8,128)S(1)} custom-call(f32[128,128]{1,0:T(8,128)S(1)} %cholesky.586), custom_call_target="Cholesky" | custom-call | tf_op jit(solution)/shard_map/jit(cholesky)/cholesky | solution.py:11
  192.8 9.8 %custom-call.68 = f32[1,128,128]{1,2,0:T(8,128)S(1)} custom-call(f32[1,128,128]{2,1,0:T(8,128)S(1)} %get-tuple-element.38), custom_call_target="InvertDiagBlocksLowerTriangular" | custom-call | tf_op jit(solution)/shard_map/jit(cholesky)/cholesky | solution.py:11
  206.3 11.7 %cholesky.485 = f32[128,128]{1,0:T(8,128)S(1)} custom-call(f32[128,128]{1,0:T(8,128)S(1)} %cholesky.591), custom_call_target="Cholesky" | custom-call | tf_op jit(solution)/shard_map/jit(cholesky)/cholesky | solution.py:11
  218.7 9.8 %custom-call.69 = f32[1,128,128]{1,2,0:T(8,128)S(1)} custom-call(f32[1,128,128]{2,1,0:T(8,128)S(1)} %get-tuple-element.35), custom_call_target="InvertDiagBlocksLowerTriangular" | custom-call | tf_op jit(solution)/shard_map/jit(cholesky)/cholesky | solution.py:11
  232.0 11.7 %cholesky.504 = f32[128,128]{1,0:T(8,128)S(1)} custom-call(f32[128,128]{1,0:T(8,128)S(1)} %cholesky.596), custom_call_target="Cholesky" | custom-call | tf_op jit(solution)/shard_map/jit(cholesky)/cholesky | solution.py:11
  244.4 10.2 %custom-call.70 = f32[1,128,128]{1,2,0:T(8,128)S(1)} custom-call(f32[1,128,128]{2,1,0:T(8,128)S(1)} %get-tuple-element.32), custom_call_target="InvertDiagBlocksLowerTriangular" | custom-call | tf_op jit(solution)/shard_map/jit(cholesky)/cholesky | solution.py:11
  257.9 11.7 %cholesky.524 = f32[128,128]{1,0:T(8,128)S(1)} custom-call(f32[128,128]{1,0:T(8,128)S(1)} %cholesky.601), custom_call_target="Cholesky" | custom-call | tf_op jit(solution)/shard_map/jit(cholesky)/cholesky | solution.py:11
  270.2 9.8 %custom-call.71 = f32[1,128,128]{1,2,0:T(8,128)S(1)} custom-call(f32[1,128,128]{2,1,0:T(8,128)S(1)} %get-tuple-element.29), custom_call_target="InvertDiagBlocksLowerTriangular" | custom-call | tf_op jit(solution)/shard_map/jit(cholesky)/cholesky | solution.py:11
  283.0 11.9 %cholesky.544 = f32[128,128]{1,0:T(8,128)S(1)} custom-call(f32[128,128]{1,0:T(8,128)S(1)} %cholesky.606), custom_call_target="Cholesky" | custom-call | tf_op jit(solution)/shard_map/jit(cholesky)/cholesky | solution.py:11
  295.5 9.8 %custom-call.72 = f32[1,128,128]{1,2,0:T(8,128)S(1)} custom-call(f32[1,128,128]{2,1,0:T(8,128)S(1)} %get-tuple-element.26), custom_call_target="InvertDiagBlocksLowerTriangular" | custom-call | tf_op jit(solution)/shard_map/jit(cholesky)/cholesky | solution.py:11
  308.0 11.7 %cholesky.562 = f32[128,128]{1,0:T(8,128)S(1)} custom-call(f32[128,128]{1,0:T(8,128)S(1)} %convolution_subtract_fusion.6), custom_call_target="Cholesky" | custom-call | tf_op jit(solution)/shard_map/jit(cholesky)/cholesky | solution.py:11
  329.9 4.8 select_select_fusion
  334.7 22.5 %while.1 = (s32[]{:T(128)}, f32[1024,1024]{1,0:T(8,128)}, s32[8,2]{0,1:T(2,128)S(1)}, f32[8,128,128]{2,1,0:T(8,128)S(1)}, s32[]{:T(128)}) while((s32[]{:T(128)}, f32[1024,1024]{1,0:T(8,128)}, s32[8,2]{0,1:T(2,128)S(1)}, f32[8,128,128]{2,1,0:T(8,128)S(1)}, s32[]{:T(128)}) %tuple.56), condition=%wide.while_cond, body=%wide.while_body.sunk | while | flops 2 | bytes 131189 | solution.py:13
  357.2 78.8 %custom-call.73 = f32[8,128,128]{1,2,0:T(8,128)S(1)} custom-call(f32[8,128,128]{2,1,0:T(8,128)S(1)} %get-tuple-element.12), custom_call_target="InvertDiagBlocksLowerTriangular" | custom-call | tf_op jit(solution)/shard_map/jit(_solve_triangular)/triangular_solve | solution.py:13
  436.0 365.3 %reduce-scatter.5.cloned.1.call-done = f32[8,1024]{1,0:T(8,128)} async-done(((f32[1024,1024]{1,0:T(8,128)}), f32[8,1024]{1,0:T(8,128)}) %reduce-scatter.5.cloned.1.call-update) | async-done | bytes 32784 | tf_op jit(solution)/shard_map/reduce_scatter | solution.py:27
  823.0 70.4 %psum.7 = f32[1024]{0:T(1024)S(1)} all-reduce(f32[1024]{0:T(1024)S(1)} %multiply_reduce_fusion), channel_id=1, replica_groups=mesh['dp'=32,'tensor'=4] {'dp','tensor'}, use_global_device_ids=true, to_apply=%region_19.20 | all-reduce | flops 1024 | bytes 8192 | tf_op jit(solution)/shard_map/psum | solution.py:38
  (135 shorter events, 95.8 us)
Async XLA Ops:
  7.4 92.3 %all-gather.2.cloned.1.call-start = ((), (), s32[]{:S(2)}) async-start(), calls=%async_computation.2 | async-start | bytes 2113536 | tf_op jit(solution)/shard_map/all_gather | solution.py:24
  8.1 152.6 %reduce-scatter.3.cloned.1.call-start = ((), (), s32[]{:S(2)}) async-start(), calls=%async_computation.3 | async-start | bytes 5242880 | tf_op jit(solution)/shard_map/reduce_scatter | solution.py:18
  21.9 779.3 %reduce-scatter.5.cloned.1.call-start = ((), (), s32[]{:S(2)}) async-start(), calls=%async_computation.4 | async-start | bytes 4227072 | tf_op jit(solution)/shard_map/reduce_scatter | solution.py:27
  104.2 2.0 copy-start
  118.9 2.0 copy-start.1
  120.8 39.9 %copy-start.2 = (bf16[1024,1024]{1,0:T(8,128)(2,1)S(1)}, bf16[1024,1024]{1,0:T(8,128)(2,1)}, u32[]{:S(2)}) copy-start(bf16[1024,1024]{1,0:T(8,128)(2,1)} %all-gather.2.cloned.1.call-done) | copy-start | bytes 6291460
Sparse Core Ops, SparseCore 0:
  11.2 88.4 all-gather.1
  166.7 634.4 reduce-scatter.4
Sparse Core Ops, SparseCore 1:
  22.0 50.3 reduce-scatter.2
where the time goes:
time: 908 us; the launch traced here: 902 us
  waiting for transfers between devices  444 us (49%)
  other arithmetic  263 us (29%)
  blocking collectives  70.4 us (8%)
  matrix products  68.9 us (8%)
  local copies, waits for them, and re-layouts  34.8 us (4%)
  between operations  20.4 us (2%)
    reduce_scatter x1, waiting for transfers between devices, shards(): lax.psum_scatter(lax.dot_general(summed, squared, (((0,), (0,)), ((), ())...  365 us
    another operation x30, other arithmetic, solve_rows(): lower = jnp.linalg.cholesky(hadamard)  172 us
    another operation x3, other arithmetic, solve_rows(): jax.scipy.linalg.solve_triangular(lower, first, lower=True, trans=1)  83.6 us
    all_gather x1, waiting for transfers between devices, shards(): whole_factor = lax.all_gather(factor, ('dp', 'tensor'), axis=0, tiled=True)  77.6 us
    psum x1, blocking collectives, shards(): lax.psum(jnp.sum(updated * updated, axis=0), ('dp', 'tensor'))  70.4 us
    another operation x14, matrix products, solve_rows(): lower = jnp.linalg.cholesky(hadamard)  23.3 us
    another operation x24, local copies, waits for them, and re-layouts  22.3 us
  transfers between devices with their start and end apart: 3, of which 2 were waited for; matrix products, arithmetic and copies ran while one was open for 37% of the time, Pallas kernels for 0%

commit v1 on v0

--- a/solution.py
+++ b/solution.py
@@ -15,6 +15,10 @@
 
 
 def shards(activations, whitening, factor):
+
+    def rest_files(slab_in, chip_axis):
+        return jnp.sum(lax.all_gather(slab_in, chip_axis), 0)
+
     summed = lax.psum_scatter(
         jnp.dot(activations, whitening, preferred_element_type=jnp.float32).astype(jnp.bfloat16),
         "tensor",
@@ -35,7 +39,7 @@
     gram = jnp.dot(whole_factor.T, whole_factor, preferred_element_type=jnp.float32)
     hadamard = gram * gram + ridge_shift * jnp.eye(gram.shape[0], dtype=jnp.float32)
     updated = solve_rows(moment_rows, hadamard)
-    column_total = lax.psum(jnp.sum(updated * updated, axis=0), ("dp", "tensor"))
+    column_total = rest_files(jnp.sum(updated * updated, axis=0), ("dp", "tensor"))
     scale = jnp.sqrt(column_total / whole_factor.shape[0] + epsilon)
     return updated / scale[None, :]
 

time: 908 us -> 896 us (0.987)
  blocking collectives: 70.4 us -> 58 us
    psum x1 -> x0, blocking collectives: 70.4 us -> none  [shards(): lax.psum(jnp.sum(updated * updated, axis=0), ('dp', 'tensor'))]
    all_gather x0 -> x1, blocking collectives: none -> 58 us  [rest_files(): return jnp.sum(lax.all_gather(slab_in, chip_axis), 0)]
  transfers between devices with their start and end apart: 3 -> 3, of which waited for: 2 -> 2; matrix products, arithmetic and copies ran while one was open for 37% -> 38% of each run, Pallas kernels for 0% -> 0%
where the time goes in v1:
time: 896 us; the launch traced here: 889 us
  waiting for transfers between devices  444 us (50%)
  other arithmetic  264 us (29%)
  matrix products  68.7 us (8%)
  blocking collectives  58 us (6%)
  local copies, waits for them, and re-layouts  34.7 us (4%)
  between operations  20.4 us (2%)
    reduce_scatter x1, waiting for transfers between devices, shards(): lax.psum_scatter(lax.dot_general(summed, squared, (((0,), (0,)), ((), ())...  365 us
    another operation x30, other arithmetic, solve_rows(): lower = jnp.linalg.cholesky(hadamard)  172 us
    another operation x3, other arithmetic, solve_rows(): jax.scipy.linalg.solve_triangular(lower, first, lower=True, trans=1)  83.6 us
    all_gather x1, waiting for transfers between devices, shards(): whole_factor = lax.all_gather(factor, ('dp', 'tensor'), axis=0, tiled=True)  77.6 us
    all_gather x1, blocking collectives, rest_files(): return jnp.sum(lax.all_gather(slab_in, chip_axis), 0)  58 us
    another operation x14, matrix products, solve_rows(): lower = jnp.linalg.cholesky(hadamard)  23.3 us
    another operation x24, local copies, waits for them, and re-layouts  22.3 us
  transfers between devices with their start and end apart: 3, of which 2 were waited for; matrix products, arithmetic and copies ran while one was open for 38% of the time, Pallas kernels for 0%

profile of v1, /device:TPU:1, one launch (start us, length us, event | category | flops | bytes accessed | tf_op | source)
XLA Modules:
  0.0 889.4 jit_solution(5222833926832703643)
XLA Ops:
  8.1 13.8 %convolution_convert_fusion = bf16[2048,1024]{1,0:T(8,128)(2,1)} fusion(bf16[2048,2048]{1,0:T(8,128)(2,1)} %param.3, bf16[2048,1024]{1,0:T(8,128)(2,1)} %param.4), kind=kOutput, calls=%fused_computation.8 | convolution fusion | flops 8592031744 | bytes 16777216 | tf_op jit(solution)/shard_map/dot_general | solution.py:23
  22.0 77.6 %all-gather.3.cloned.1.call-done = bf16[1024,1024]{1,0:T(8,128)(2,1)} async-done(((bf16[8,1024]{1,0:T(8,128)(2,1)}), bf16[1024,1024]{1,0:T(8,128)(2,1)}) %all-gather.3.cloned.1.call-update) | async-done | bytes 2097168 | tf_op jit(solution)/shard_map/all_gather | solution.py:28
  108.6 5.6 copy.6
  120.7 11.7 %cholesky.222 = f32[128,128]{1,0:T(8,128)S(1)} custom-call(f32[128,128]{1,0:T(8,128)S(1)} %cholesky.577), custom_call_target="Cholesky" | custom-call | tf_op jit(solution)/shard_map/jit(cholesky)/cholesky | solution.py:11
  134.9 9.8 %custom-call.66 = f32[1,128,128]{1,2,0:T(8,128)S(1)} custom-call(f32[1,128,128]{2,1,0:T(8,128)S(1)} %get-tuple-element.44), custom_call_target="InvertDiagBlocksLowerTriangular" | custom-call | tf_op jit(solution)/shard_map/jit(cholesky)/cholesky | solution.py:11
  148.7 12.2 %cholesky.243 = f32[128,128]{1,0:T(8,128)S(1)} custom-call(f32[128,128]{1,0:T(8,128)S(1)} %cholesky.581), custom_call_target="Cholesky" | custom-call | tf_op jit(solution)/shard_map/jit(cholesky)/cholesky | solution.py:11
  160.9 5.9 fusion.1
  167.4 9.8 %custom-call.67 = f32[1,128,128]{1,2,0:T(8,128)S(1)} custom-call(f32[1,128,128]{2,1,0:T(8,128)S(1)} %get-tuple-element.41), custom_call_target="InvertDiagBlocksLowerTriangular" | custom-call | tf_op jit(solution)/shard_map/jit(cholesky)/cholesky | solution.py:11
  180.6 11.7 %cholesky.466 = f32[128,128]{1,0:T(8,128)S(1)} custom-call(f32[128,128]{1,0:T(8,128)S(1)} %cholesky.586), custom_call_target="Cholesky" | custom-call | tf_op jit(solution)/shard_map/jit(cholesky)/cholesky | solution.py:11
  193.0 9.8 %custom-call.68 = f32[1,128,128]{1,2,0:T(8,128)S(1)} custom-call(f32[1,128,128]{2,1,0:T(8,128)S(1)} %get-tuple-element.38), custom_call_target="InvertDiagBlocksLowerTriangular" | custom-call | tf_op jit(solution)/shard_map/jit(cholesky)/cholesky | solution.py:11
  206.5 11.7 %cholesky.485 = f32[128,128]{1,0:T(8,128)S(1)} custom-call(f32[128,128]{1,0:T(8,128)S(1)} %cholesky.591), custom_call_target="Cholesky" | custom-call | tf_op jit(solution)/shard_map/jit(cholesky)/cholesky | solution.py:11
  218.8 9.8 %custom-call.69 = f32[1,128,128]{1,2,0:T(8,128)S(1)} custom-call(f32[1,128,128]{2,1,0:T(8,128)S(1)} %get-tuple-element.35), custom_call_target="InvertDiagBlocksLowerTriangular" | custom-call | tf_op jit(solution)/shard_map/jit(cholesky)/cholesky | solution.py:11
  232.1 11.7 %cholesky.504 = f32[128,128]{1,0:T(8,128)S(1)} custom-call(f32[128,128]{1,0:T(8,128)S(1)} %cholesky.596), custom_call_target="Cholesky" | custom-call | tf_op jit(solution)/shard_map/jit(cholesky)/cholesky | solution.py:11
  244.5 10.0 %custom-call.70 = f32[1,128,128]{1,2,0:T(8,128)S(1)} custom-call(f32[1,128,128]{2,1,0:T(8,128)S(1)} %get-tuple-element.32), custom_call_target="InvertDiagBlocksLowerTriangular" | custom-call | tf_op jit(solution)/shard_map/jit(cholesky)/cholesky | solution.py:11
  257.8 11.7 %cholesky.524 = f32[128,128]{1,0:T(8,128)S(1)} custom-call(f32[128,128]{1,0:T(8,128)S(1)} %cholesky.601), custom_call_target="Cholesky" | custom-call | tf_op jit(solution)/shard_map/jit(cholesky)/cholesky | solution.py:11
  270.2 9.8 %custom-call.71 = f32[1,128,128]{1,2,0:T(8,128)S(1)} custom-call(f32[1,128,128]{2,1,0:T(8,128)S(1)} %get-tuple-element.29), custom_call_target="InvertDiagBlocksLowerTriangular" | custom-call | tf_op jit(solution)/shard_map/jit(cholesky)/cholesky | solution.py:11
  283.0 12.1 %cholesky.544 = f32[128,128]{1,0:T(8,128)S(1)} custom-call(f32[128,128]{1,0:T(8,128)S(1)} %cholesky.606), custom_call_target="Cholesky" | custom-call | tf_op jit(solution)/shard_map/jit(cholesky)/cholesky | solution.py:11
  295.7 9.8 %custom-call.72 = f32[1,128,128]{1,2,0:T(8,128)S(1)} custom-call(f32[1,128,128]{2,1,0:T(8,128)S(1)} %get-tuple-element.26), custom_call_target="InvertDiagBlocksLowerTriangular" | custom-call | tf_op jit(solution)/shard_map/jit(cholesky)/cholesky | solution.py:11
  308.2 11.7 %cholesky.562 = f32[128,128]{1,0:T(8,128)S(1)} custom-call(f32[128,128]{1,0:T(8,128)S(1)} %convolution_subtract_fusion.6), custom_call_target="Cholesky" | custom-call | tf_op jit(solution)/shard_map/jit(cholesky)/cholesky | solution.py:11
  330.0 4.8 select_select_fusion
  334.9 22.5 %while.1 = (s32[]{:T(128)}, f32[1024,1024]{1,0:T(8,128)}, s32[8,2]{0,1:T(2,128)S(1)}, f32[8,128,128]{2,1,0:T(8,128)S(1)}, s32[]{:T(128)}) while((s32[]{:T(128)}, f32[1024,1024]{1,0:T(8,128)}, s32[8,2]{0,1:T(2,128)S(1)}, f32[8,128,128]{2,1,0:T(8,128)S(1)}, s32[]{:T(128)}) %tuple.56), condition=%wide.while_cond, body=%wide.while_body.sunk | while | flops 2 | bytes 131189 | solution.py:13
  357.4 78.8 %custom-call.73 = f32[8,128,128]{1,2,0:T(8,128)S(1)} custom-call(f32[8,128,128]{2,1,0:T(8,128)S(1)} %get-tuple-element.12), custom_call_target="InvertDiagBlocksLowerTriangular" | custom-call | tf_op jit(solution)/shard_map/jit(_solve_triangular)/triangular_solve | solution.py:13
  436.1 365.3 %reduce-scatter.5.cloned.1.call-done = f32[8,1024]{1,0:T(8,128)} async-done(((f32[1024,1024]{1,0:T(8,128)}), f32[8,1024]{1,0:T(8,128)}) %reduce-scatter.5.cloned.1.call-update) | async-done | bytes 32784 | tf_op jit(solution)/shard_map/reduce_scatter | solution.py:31
  823.0 58.0 %all-gather = f32[131072]{0:T(1024)S(1)} all-gather(f32[1024]{0:T(1024)S(1)} %multiply_reduce_fusion), channel_id=2, replica_groups=mesh['dp'=32,'tensor'=4] {'dp','tensor'}, dimensions={0}, use_global_device_ids=true | all-gather | bytes 528384 | tf_op jit(solution)/shard_map/all_gather | solution.py:20
  (137 shorter events, 95.7 us)
Async XLA Ops:
  7.4 92.3 %all-gather.3.cloned.1.call-start = ((), (), s32[]{:S(2)}) async-start(), calls=%async_computation.2 | async-start | bytes 2113536 | tf_op jit(solution)/shard_map/all_gather | solution.py:28
  8.1 152.8 %reduce-scatter.3.cloned.1.call-start = ((), (), s32[]{:S(2)}) async-start(), calls=%async_computation.3 | async-start | bytes 5242880 | tf_op jit(solution)/shard_map/reduce_scatter | solution.py:22
  21.9 779.5 %reduce-scatter.5.cloned.1.call-start = ((), (), s32[]{:S(2)}) async-start(), calls=%async_computation.4 | async-start | bytes 4227072 | tf_op jit(solution)/shard_map/reduce_scatter | solution.py:31
  104.2 2.0 copy-start
  118.7 2.0 copy-start.1
  120.7 40.2 %copy-start.2 = (bf16[1024,1024]{1,0:T(8,128)(2,1)S(1)}, bf16[1024,1024]{1,0:T(8,128)(2,1)}, u32[]{:S(2)}) copy-start(bf16[1024,1024]{1,0:T(8,128)(2,1)} %all-gather.3.cloned.1.call-done) | copy-start | bytes 6291460
Sparse Core Ops, SparseCore 0:
  11.2 88.4 all-gather.2
  166.9 634.5 reduce-scatter.4
Sparse Core Ops, SparseCore 1:
  22.0 50.3 reduce-scatter.2
